TPU v7x, 32 devices: a whole 2x2x4 slice. The times are simulated.
32 devices in a mesh: groups: 2 (over y), seq: 16 (over z, x, core).
Axes of the slice: x: 2, y: 2, z: 4, core: 2. Of those that a mesh axis runs over, the one named last changes fastest.
Arguments:
- span_frames: bfloat16 [512, 512], P(('groups', 'seq')), parts along dimension 0, may hold values from -3 to 3
- query_rows: bfloat16 [512, 512], P(('groups', 'seq')), parts along dimension 0, may hold values from -12 to 12
- key_rows: bfloat16 [16384, 512], P(('groups', 'seq')), parts along dimension 0, may hold values from -6 to 6
- context_frames: bfloat16 [16384, 512], P(('groups', 'seq')), parts along dimension 0, may hold values from -6 to 6
- key_mask: int32 [16384], P(('groups', 'seq')), parts along dimension 0, may hold values from 0 to 1, as said below
- value_weight: bfloat16 [512, 512], replicated, may hold values from -0.5 to 0.5
- out_weight: bfloat16 [512, 512], replicated, may hold values from -0.25 to 0.25
- expand_weight: bfloat16 [512, 1024], replicated, may hold values from -0.25 to 0.25
- depth_weight: float32 [31, 512], replicated, may hold values from -1 to 1
- norm_scale: float32 [512], replicated, may hold values from 0.5 to 2
- norm_shift: float32 [512], replicated, may hold values from -3 to 3
- project_weight: bfloat16 [512, 512], replicated, may hold values from -0.25 to 0.25
Outputs:
- layer_out: bfloat16 [512, 512], P(('groups', 'seq')), parts along dimension 0
There are 2 independent parts, one for each index of `groups`. A program takes and returns all parts, laid end to end along the dimension named above; an argument that names none is the same for every part. Nothing has to cross between parts.
Inputs may be any that keep to these rules, and one draw needn't show every extreme that they name: `key_mask`: within each block of 512 frames held by one index of seq, the real frames come first and there is at least one.
All inputs are finite; a program needn't handle non-finite values.
Results may differ from a plain program's by a relative error of at most 0.013.
Values may be sent and summed in bfloat16 or wider, within the bound.
A program may use at most 384 MiB of HBM per device.

v0:
```python
import math
import jax
import jax.numpy as jnp
from jax import lax
from jax.sharding import PartitionSpec as P

HEADS = 8


def combined_all(value, axis, join):
    pieces = jax.tree.map(lambda part: lax.all_gather(part, axis), value)
    head = jax.tree.map(lambda part: part[0], pieces)
    tail = jax.tree.map(lambda part: part[1:], pieces)
    so_far, _ = lax.scan(lambda so_far, section: (join(so_far, section), None), head, tail)
    return so_far


def with_halo(block, sides, width):
    for axis, dim in sides:
        count = lax.axis_size(axis)
        forward = [(i, i + 1) for i in range(count - 1)]
        backward = [(target, source) for source, target in forward]
        low = lax.ppermute(
            lax.slice_in_dim(block, block.shape[dim] - width, None, axis=dim), axis, forward
        )
        high = lax.ppermute(lax.slice_in_dim(block, 0, width, axis=dim), axis, backward)
        block = jnp.concatenate([low, block, high], axis=dim)
    return block


def combine_partial(first_part, second_part):
    out_first, lse_first = first_part
    out_second, lse_second = second_part
    width = out_first.shape[1] // lse_first.shape[0]
    joint = jnp.logaddexp(lse_first, lse_second)
    share_first = jnp.repeat(jnp.exp(lse_first - joint).T, width, axis=1)
    share_second = jnp.repeat(jnp.exp(lse_second - joint).T, width, axis=1)
    return (out_first * share_first + out_second * share_second, joint)


def body(
    span_frames,
    query_rows,
    key_rows,
    context_frames,
    key_mask,
    value_weight,
    out_weight,
    expand_weight,
    depth_weight,
    norm_scale,
    norm_shift,
    project_weight,
):
    width = key_rows.shape[1]
    head_dim = width // HEADS
    scale = 1.0 / math.sqrt(head_dim)
    values = jnp.dot(context_frames, value_weight, preferred_element_type=jnp.float32).astype(
        jnp.bfloat16
    )
    key_heads = key_rows.reshape(key_rows.shape[0], HEADS, head_dim)
    value_heads = values.reshape(values.shape[0], HEADS, head_dim)
    valid = key_mask > 0
    gathered = lax.all_gather(query_rows, "seq", axis=0, tiled=True)
    own_rows = query_rows.shape[0]
    total_rows = gathered.shape[0]
    block = min(512, total_rows)
    blocks = total_rows // block
    query_blocks = gathered.reshape(blocks, block, HEADS, head_dim)

    def block_scores(query_block):
        scores = (
            jnp.einsum("bhd,khd->hbk", query_block, key_heads, preferred_element_type=jnp.float32)
            * scale
        )
        return jnp.where(valid[None, None, :], scores, -1e30)

    def weighted(scores, shift_rows):
        weights = jnp.exp(scores - shift_rows[:, :, None])
        total = jnp.sum(weights, axis=2)
        numer = jnp.einsum(
            "hbk,khd->bhd",
            weights.astype(jnp.bfloat16),
            value_heads,
            preferred_element_type=jnp.float32,
        )
        return (numer.reshape(numer.shape[0], width), total)

    def merged_block(query_block):
        scores = block_scores(query_block)
        top = jnp.max(scores, axis=2)
        numer, total = weighted(scores, top)
        partial_value = numer / jnp.repeat(total.T, head_dim, axis=1)
        partial_lse = top + jnp.log(total)
        return combined_all((partial_value, partial_lse), "seq", combine_partial)

    merged, merged_lse = lax.map(merged_block, query_blocks)
    merged = merged.reshape(total_rows, width)
    first_row = lax.axis_index("seq") * own_rows
    attended = lax.dynamic_slice_in_dim(merged, first_row, own_rows, 0).astype(jnp.bfloat16)
    wide = span_frames.astype(jnp.float32) + jnp.dot(
        attended, out_weight, preferred_element_type=jnp.float32
    )
    mixed = wide.astype(jnp.bfloat16)
    stream = mixed.astype(jnp.float32)
    centre = jnp.mean(stream, axis=1, keepdims=True)
    spread = jnp.mean((stream - centre) ** 2, axis=1, keepdims=True)
    normed = ((stream - centre) / jnp.sqrt(spread + 1e-05)).astype(jnp.bfloat16)
    expanded = jnp.dot(normed, expand_weight, preferred_element_type=jnp.float32)
    gated = (expanded[:, :width] * jax.nn.sigmoid(expanded[:, width:])).astype(jnp.bfloat16)
    reach = depth_weight.shape[0] // 2
    padded = with_halo(gated, (("seq", 0),), reach).astype(jnp.float32)
    conv = jnp.zeros((own_rows, width), jnp.float32)
    for offset in range(depth_weight.shape[0]):
        conv = conv + padded[offset : offset + own_rows] * depth_weight[offset][None, :]
    normal_conv = conv * norm_scale[None, :] + norm_shift[None, :]
    activated = (normal_conv * jax.nn.sigmoid(normal_conv)).astype(jnp.bfloat16)
    return (stream + jnp.dot(activated, project_weight, preferred_element_type=jnp.float32)).astype(
        jnp.bfloat16
    )


def solution(mesh):
    in_specs = (
        P(("groups", "seq"), None),
        P(("groups", "seq"), None),
        P(("groups", "seq"), None),
        P(("groups", "seq"), None),
        P(("groups", "seq")),
        P(),
        P(),
        P(),
        P(),
        P(),
        P(),
        P(),
    )
    out_specs = P(("groups", "seq"), None)
    return jax.shard_map(body, mesh=mesh, in_specs=in_specs, out_specs=out_specs, check_vma=False)
```

profile of v0, /device:TPU:3, one launch (start us, length us, event | category | flops | bytes accessed | tf_op | source)
XLA Modules:
  0.0 159.9 jit_solution(10683933736203446552)
XLA Ops:
  6.5 0.8 broadcast_compare_fusion
  7.3 19.4 %all_gather.15 = bf16[256,512]{1,0:T(8,128)(2,1)S(1)} all-gather(bf16[16,512]{1,0:T(8,128)(2,1)} %param.15), channel_id=1, replica_groups=mesh['groups'=2,'seq'=16] {'seq'}, dimensions={0}, use_global_device_ids=true | all-gather | bytes 278528 | tf_op jit(solution)/shard_map/all_gather | solution.py:64
  26.8 1.3 copy.21
  28.1 0.8 fusion.5
  29.0 1.2 fusion.6
  30.2 0.5 convolution_convert_fusion
  30.7 1.1 fusion.17
  31.8 1.0 copy.22
  32.9 22.3 %all-gather = f32[128,256]{1,0:T(8,128)S(1)} all-gather(f32[8,256]{1,0:T(8,128)S(1)} %log_add_fusion), channel_id=2, replica_groups=mesh['groups'=2,'seq'=16] {'seq'}, dimensions={0}, use_global_device_ids=true | all-gather | bytes 139264 | tf_op jit(solution)/shard_map/while/body/eval_jaxpr/all_gather | solution.py:11
  55.2 52.4 %all-gather.3.cloned.1.call-done = f32[16,256,512]{2,1,0:T(8,128)} async-done(((f32[1,256,512]{2,1,0:T(8,128)}), f32[16,256,512]{2,1,0:T(8,128)}) %all-gather.3.cloned.1.call-update) | async-done | bytes 8388624 | tf_op jit(solution)/shard_map/while/body/eval_jaxpr/all_gather | solution.py:11
  107.6 1.1 slice_bitcast_fusion
  108.9 7.6 %slice.289 = f32[15,256,512]{2,1,0:T(8,128)} slice(f32[16,256,512]{2,1,0:T(8,128)} %all-gather.3.cloned.1.call-done), slice={[1:16], [0:256], [0:512]} | slice | bytes 15728640 | tf_op jit(solution)/shard_map/while/body/eval_jaxpr/slice | solution.py:13
  116.5 23.7 %while.19 = (s32[]{:T(128)}, f32[256,512]{0,1:T(8,128)S(1)}, f32[8,256]{1,0:T(8,128)S(1)}, f32[15,8,256]{2,1,0:T(8,128)S(1)}, f32[15,256,512]{2,1,0:T(8,128)}, /*index=5*/s32[]{:T(128)}) while((s32[]{:T(128)}, f32[256,512]{0,1:T(8,128)S(1)}, f32[8,256]{1,0:T(8,128)S(1)}, f32[15,8,256]{2,1,0:T(8,128)S(1)}, f32[15,256,512]{2,1,0:T(8,128)}, ...), condition=%wide.region_3.4_spmd, body=%wide.region_2.3_spmd.sunk | while | flops 413698 | bytes 3743825 | solution.py:14
  116.6 1.1 constant_dynamic-slice_fusion.2
  118.2 1.1 constant_dynamic-slice_fusion.2
  119.8 1.1 constant_dynamic-slice_fusion.2
  121.3 1.1 constant_dynamic-slice_fusion.2
  122.9 1.1 constant_dynamic-slice_fusion.2
  124.5 1.1 constant_dynamic-slice_fusion.2
  126.1 1.1 constant_dynamic-slice_fusion.2
  127.6 1.1 constant_dynamic-slice_fusion.2
  129.2 1.1 constant_dynamic-slice_fusion.2
  130.8 1.1 constant_dynamic-slice_fusion.2
  132.4 1.1 constant_dynamic-slice_fusion.2
  133.9 1.1 constant_dynamic-slice_fusion.2
  135.5 1.1 constant_dynamic-slice_fusion.2
  137.1 1.1 constant_dynamic-slice_fusion.2
  138.7 1.1 constant_dynamic-slice_fusion.2
  141.2 3.9 %collective-permute-start = (bf16[15,512]{1,0:T(8,128)(2,1)S(1)}, bf16[15,512]{1,0:T(8,128)(2,1)S(1)}, u32[]{:S(2)}, u32[]{:S(2)}) collective-permute-start(bf16[15,512]{1,0:T(8,128)(2,1)S(1)} %get-tuple-element.99), channel_id=1, source_target_pairs={{0,1},{1,2},{2,3},{3,4},{4,5},{5,6},{6,7},{7,8},{8,9},{9,10},{10,1... | collective-permute-start | bytes 46088 | tf_op jit(solution)/shard_map/ppermute | solution.py:23
  145.1 1.9 %collective-permute-start.1 = (bf16[15,512]{1,0:T(8,128)(2,1)S(1)}, bf16[15,512]{1,0:T(8,128)(2,1)S(1)}, u32[]{:S(2)}, u32[]{:S(2)}) collective-permute-start(bf16[15,512]{1,0:T(8,128)(2,1)S(1)} %get-tuple-element.100), channel_id=1, source_target_pairs={{1,0},{2,1},{3,2},{4,3},{5,4},{6,5},{7,6},{8,7},{9,8},{10,9},{11,1... | collective-permute-start | bytes 46088 | tf_op jit(solution)/shard_map/ppermute | solution.py:26
  147.0 4.0 %collective-permute-done.1 = bf16[15,512]{1,0:T(8,128)(2,1)S(1)} collective-permute-done((bf16[15,512]{1,0:T(8,128)(2,1)S(1)}, bf16[15,512]{1,0:T(8,128)(2,1)S(1)}, u32[]{:S(2)}, u32[]{:S(2)}) %collective-permute-start.1) | collective-permute-done | bytes 15392 | tf_op jit(solution)/shard_map/ppermute | solution.py:26
  151.1 2.0 %fusion.16 = bf16[16,512]{1,0:T(8,128)(2,1)} fusion(f32[16,512]{1,0:T(8,128)S(1)} %get-tuple-element.104, bf16[512,512]{1,0:T(8,128)(2,1)} %param.25, f32[46,512]{1,0:T(8,128)S(1)} %maximum_convert_fusion, f32[512]{0:T(512)S(1)} %copy-done.6, f32[512]{0:T(512)S(1)} %copy-done.7, f32[512]{0:T(512)S(1)} %bitcast.130, f32[512]{0:T(512)S(1)} %bitcast.131, ...), kind=kOutput, calls=%fused_computation.26 | convolution fusion | flops 8962048 | bytes 1656832 | tf_op jit(solution)/shard_map/dot_general | solution.py:118
  (94 shorter events, 8.1 us)
Async XLA Ops:
  6.5 134.3 %copy-start = (bf16[512,1024]{1,0:T(8,128)(2,1)S(1)}, bf16[512,1024]{1,0:T(8,128)(2,1)}, u32[]{:S(2)}) copy-start(bf16[512,1024]{1,0:T(8,128)(2,1)} %param.21) | copy-start | bytes 3145732
  6.5 101.1 %all-gather.3.cloned.1.call-start = ((), (), s32[]{:S(2)}) async-start(), calls=%async_computation | async-start | bytes 8912896 | tf_op jit(solution)/shard_map/while/body/eval_jaxpr/all_gather | solution.py:11
  28.1 2.1 %copy-start.1 = (bf16[512,512]{1,0:T(8,128)(2,1)S(1)}, bf16[512,512]{1,0:T(8,128)(2,1)}, u32[]{:S(2)}) copy-start(bf16[512,512]{1,0:T(8,128)(2,1)} %param.17) | copy-start | bytes 1572868
  28.1 2.1 %copy-start.2 = (bf16[512,512]{1,0:T(8,128)(2,1)S(1)}, bf16[512,512]{1,0:T(8,128)(2,1)}, u32[]{:S(2)}) copy-start(bf16[512,512]{1,0:T(8,128)(2,1)} %param.19) | copy-start | bytes 1572868
  30.7 24.5 %copy-start.4 = (f32[31,512]{1,0:T(8,128)S(1)}, f32[31,512]{1,0:T(8,128)}, u32[]{:S(2)}) copy-start(f32[31,512]{1,0:T(8,128)} %param.22) | copy-start | bytes 190468
  116.5 23.7 %copy-start.3 = (bf16[512,512]{1,0:T(8,128)(2,1)S(1)}, bf16[512,512]{1,0:T(8,128)(2,1)}, u32[]{:S(2)}) copy-start(bf16[512,512]{1,0:T(8,128)(2,1)} %param.20) | copy-start | bytes 1572868
  116.5 23.7 %copy-start.5 = (bf16[16,512]{1,0:T(8,128)(2,1)S(1)}, bf16[16,512]{1,0:T(8,128)(2,1)}, u32[]{:S(2)}) copy-start(bf16[16,512]{1,0:T(8,128)(2,1)} %param.14) | copy-start | bytes 49156
  116.5 34.6 %copy-start.6 = (f32[512]{0:T(512)S(1)}, f32[512]{0:T(512)}, u32[]{:S(2)}) copy-start(f32[512]{0:T(512)} %param.24) | copy-start | bytes 6148
  116.5 34.6 %copy-start.7 = (f32[512]{0:T(512)S(1)}, f32[512]{0:T(512)}, u32[]{:S(2)}) copy-start(f32[512]{0:T(512)} %param.23) | copy-start | bytes 6148
  141.2 5.9 %collective-permute-start = (bf16[15,512]{1,0:T(8,128)(2,1)S(1)}, bf16[15,512]{1,0:T(8,128)(2,1)S(1)}, u32[]{:S(2)}, u32[]{:S(2)}) collective-permute-start(bf16[15,512]{1,0:T(8,128)(2,1)S(1)} %get-tuple-element.99), channel_id=1, source_target_pairs={{0,1},{1,2},{2,3},{3,4},{4,5},{5,6},{6,7},{7,8},{8,9},{9,10},{10,1... | collective-permute-start | bytes 46088 | tf_op jit(solution)/shard_map/ppermute | solution.py:23
  145.1 6.0 %collective-permute-start.1 = (bf16[15,512]{1,0:T(8,128)(2,1)S(1)}, bf16[15,512]{1,0:T(8,128)(2,1)S(1)}, u32[]{:S(2)}, u32[]{:S(2)}) collective-permute-start(bf16[15,512]{1,0:T(8,128)(2,1)S(1)} %get-tuple-element.100), channel_id=1, source_target_pairs={{1,0},{2,1},{3,2},{4,3},{5,4},{6,5},{7,6},{8,7},{9,8},{10,9},{11,1... | collective-permute-start | bytes 46088 | tf_op jit(solution)/shard_map/ppermute | solution.py:26
Sparse Core Ops, SparseCore 0:
  33.0 74.5 all-gather.2
where the time goes:
time: 161 us; the launch traced here: 160 us
  waiting for transfers between devices  56.4 us (35%)
  blocking collectives  41.6 us (26%)
  local copies, waits for them, and re-layouts  30.6 us (19%)
  between operations  13.6 us (8%)
  other arithmetic  6.08 us (4%)
  starting transfers between devices  5.84 us (4%)
  matrix products  5.07 us (3%)
    all_gather x1, waiting for transfers between devices, combined_all(): pieces = jax.tree.map(lambda part: lax.all_gather(part, axis), value)  52.4 us
    all_gather x1, blocking collectives, combined_all(): pieces = jax.tree.map(lambda part: lax.all_gather(part, axis), value)  22.3 us
    all_gather x1, blocking collectives, body(): gathered = lax.all_gather(query_rows, 'seq', axis=0, tiled=True)  19.4 us
    dynamic_slice x30, local copies, waits for them, and re-layouts, combined_all(): lax.scan(lambda so_far, section: (join(so_far, section), None), head, tail)  19.2 us
    slice x2, local copies, waits for them, and re-layouts, combined_all(): tail = jax.tree.map(lambda part: part[1:], pieces)  7.61 us
    ppermute x1, waiting for transfers between devices, with_halo(): lax.ppermute(lax.slice_in_dim(block, 0, width, axis=dim), axis, backward)  3.99 us
    ppermute x1, starting transfers between devices, with_halo(): lax.ppermute(lax.slice_in_dim(block, block.shape[dim] - width, None, axis...  3.91 us
    add x15, other arithmetic, combine_partial(): return (out_first * share_first + out_second * share_second, joint)  3.24 us
  transfers between devices with their start and end apart: 3, of which 2 were waited for; matrix products, arithmetic and copies ran while one was open for 0% of the time, Pallas kernels for 0%

commit v1 on v0

--- a/solution.py
+++ b/solution.py
@@ -5,6 +5,12 @@
 from jax.sharding import PartitionSpec as P
 
 HEADS = 8
+
+
+def gather_from_all(x, axis, dim):
+    size = lax.axis_size(axis)
+    repeats = [size if d == dim else 1 for d in range(x.ndim)]
+    return lax.all_to_all(jnp.tile(x, repeats), axis, split_axis=dim, concat_axis=dim, tiled=True)
 
 
 def combined_all(value, axis, join):
@@ -61,7 +67,7 @@
     key_heads = key_rows.reshape(key_rows.shape[0], HEADS, head_dim)
     value_heads = values.reshape(values.shape[0], HEADS, head_dim)
     valid = key_mask > 0
-    gathered = lax.all_gather(query_rows, "seq", axis=0, tiled=True)
+    gathered = gather_from_all(query_rows, "seq", 0)
     own_rows = query_rows.shape[0]
     total_rows = gathered.shape[0]
     block = min(512, total_rows)

time: 161 us -> 155 us (0.963)
  blocking collectives: 41.6 us -> 19.8 us
  starting transfers between devices: 5.84 us -> 12.5 us
  waiting for transfers between devices: 56.4 us -> 62.2 us
  local copies, waits for them, and re-layouts: 30.6 us -> 32.3 us
    all_gather x1 -> x0, blocking collectives: 19.4 us -> none  [body(): gathered = lax.all_gather(query_rows, 'seq', axis=0, tiled=True)]
    all_to_all x0 -> x1, starting transfers between devices: none -> 6.63 us  [gather_from_all(): lax.all_to_all(jnp.tile(x, repeats), axis, split_axis=dim, concat_axis=di...]
    all_to_all x0 -> x1, waiting for transfers between devices: none -> 4.82 us  [gather_from_all(): lax.all_to_all(jnp.tile(x, repeats), axis, split_axis=dim, concat_axis=di...]
    all_gather x1, blocking collectives: 22.3 us -> 19.8 us  [combined_all(): pieces = jax.tree.map(lambda part: lax.all_gather(part, axis), value)]
  transfers between devices with their start and end apart: 3 -> 4, of which waited for: 2 -> 3; matrix products, arithmetic and copies ran while one was open for 0% -> 2% of each run, Pallas kernels for 0% -> 0%
where the time goes in v1:
time: 155 us; the launch traced here: 153 us
  waiting for transfers between devices  62.2 us (40%)
  local copies, waits for them, and re-layouts  32.3 us (21%)
  blocking collectives  19.8 us (13%)
  between operations  13.6 us (9%)
  starting transfers between devices  12.5 us (8%)
  matrix products  6.22 us (4%)
  other arithmetic  6.07 us (4%)
    all_gather x1, waiting for transfers between devices, combined_all(): pieces = jax.tree.map(lambda part: lax.all_gather(part, axis), value)  53.4 us
    all_gather x1, blocking collectives, combined_all(): pieces = jax.tree.map(lambda part: lax.all_gather(part, axis), value)  19.8 us
    dynamic_slice x30, local copies, waits for them, and re-layouts, combined_all(): lax.scan(lambda so_far, section: (join(so_far, section), None), head, tail)  19.2 us
    slice x2, local copies, waits for them, and re-layouts, combined_all(): tail = jax.tree.map(lambda part: part[1:], pieces)  7.61 us
    all_to_all x1, starting transfers between devices, gather_from_all(): lax.all_to_all(jnp.tile(x, repeats), axis, split_axis=dim, concat_axis=di...  6.63 us
    all_to_all x1, waiting for transfers between devices, gather_from_all(): lax.all_to_all(jnp.tile(x, repeats), axis, split_axis=dim, concat_axis=di...  4.82 us
    ppermute x1, waiting for transfers between devices, with_halo(): lax.ppermute(lax.slice_in_dim(block, 0, width, axis=dim), axis, backward)  3.99 us
    ppermute x1, starting transfers between devices, with_halo(): lax.ppermute(lax.slice_in_dim(block, block.shape[dim] - width, None, axis...  3.91 us
  transfers between devices with their start and end apart: 4, of which 3 were waited for; matrix products, arithmetic and copies ran while one was open for 2% of the time, Pallas kernels for 0%

profile of v1, /device:TPU:3, one launch (start us, length us, event | category | flops | bytes accessed | tf_op | source)
XLA Modules:
  0.0 153.3 jit_solution(7608614088011907402)
XLA Ops:
  6.5 1.5 tile.2
  8.1 6.6 %all-to-all-start = ((bf16[16,16,512]{2,1,0:T(8,128)(2,1)}), bf16[16,16,512]{2,1,0:T(8,128)(2,1)S(1)}, u32[]{:S(2)}, u32[]{:S(2)}) async-start(bf16[16,16,512]{2,1,0:T(8,128)(2,1)} %tile.2), calls=%async_computation | async-start | bytes 524288 | tf_op jit(solution)/shard_map/all_to_all | solution.py:13
  14.7 1.3 copy.20
  16.7 1.7 %convolution_convert_fusion = bf16[512,512]{0,1:T(8,128)(2,1)S(1)} fusion(bf16[512,512]{1,0:T(8,128)(2,1)} %param.17, bf16[512,512]{1,0:T(8,128)(2,1)} %param.19), kind=kOutput, calls=%fused_computation.20 | convolution fusion | flops 268697600 | bytes 1572864 | tf_op jit(solution)/shard_map/dot_general | solution.py:64
  18.4 4.8 %all-to-all-done = bf16[16,16,512]{2,1,0:T(8,128)(2,1)S(1)} async-done(((bf16[16,16,512]{2,1,0:T(8,128)(2,1)}), bf16[16,16,512]{2,1,0:T(8,128)(2,1)S(1)}, u32[]{:S(2)}, u32[]{:S(2)}) %all-to-all-start) | async-done | bytes 262176 | tf_op jit(solution)/shard_map/all_to_all | solution.py:13
  24.2 1.3 fusion.6
  25.6 1.1 fusion.17
  26.7 1.0 copy.22
  27.8 19.8 %all-gather = f32[128,256]{1,0:T(8,128)S(1)} all-gather(f32[8,256]{1,0:T(8,128)S(1)} %log_add_fusion), channel_id=2, replica_groups=mesh['groups'=2,'seq'=16] {'seq'}, dimensions={0}, use_global_device_ids=true | all-gather | bytes 139264 | tf_op jit(solution)/shard_map/while/body/eval_jaxpr/all_gather | solution.py:17
  47.6 53.4 %all-gather.3.cloned.1.call-done = f32[16,256,512]{2,1,0:T(8,128)} async-done(((f32[1,256,512]{2,1,0:T(8,128)}), f32[16,256,512]{2,1,0:T(8,128)}) %all-gather.3.cloned.1.call-update) | async-done | bytes 8388624 | tf_op jit(solution)/shard_map/while/body/eval_jaxpr/all_gather | solution.py:17
  101.1 1.1 slice_bitcast_fusion
  102.3 7.6 %slice.289 = f32[15,256,512]{2,1,0:T(8,128)} slice(f32[16,256,512]{2,1,0:T(8,128)} %all-gather.3.cloned.1.call-done), slice={[1:16], [0:256], [0:512]} | slice | bytes 15728640 | tf_op jit(solution)/shard_map/while/body/eval_jaxpr/slice | solution.py:19
  109.9 23.7 %while.19 = (s32[]{:T(128)}, f32[256,512]{0,1:T(8,128)S(1)}, f32[8,256]{1,0:T(8,128)S(1)}, f32[15,8,256]{2,1,0:T(8,128)S(1)}, f32[15,256,512]{2,1,0:T(8,128)}, /*index=5*/s32[]{:T(128)}) while((s32[]{:T(128)}, f32[256,512]{0,1:T(8,128)S(1)}, f32[8,256]{1,0:T(8,128)S(1)}, f32[15,8,256]{2,1,0:T(8,128)S(1)}, f32[15,256,512]{2,1,0:T(8,128)}, ...), condition=%wide.region_3.4_spmd, body=%wide.region_2.3_spmd.sunk | while | flops 413698 | bytes 3743825 | solution.py:20
  110.0 1.1 constant_dynamic-slice_fusion.2
  111.6 1.1 constant_dynamic-slice_fusion.2
  113.2 1.1 constant_dynamic-slice_fusion.2
  114.8 1.1 constant_dynamic-slice_fusion.2
  116.3 1.1 constant_dynamic-slice_fusion.2
  117.9 1.1 constant_dynamic-slice_fusion.2
  119.5 1.1 constant_dynamic-slice_fusion.2
  121.1 1.1 constant_dynamic-slice_fusion.2
  122.6 1.1 constant_dynamic-slice_fusion.2
  124.2 1.1 constant_dynamic-slice_fusion.2
  125.8 1.1 constant_dynamic-slice_fusion.2
  127.4 1.1 constant_dynamic-slice_fusion.2
  128.9 1.1 constant_dynamic-slice_fusion.2
  130.5 1.1 constant_dynamic-slice_fusion.2
  132.1 1.1 constant_dynamic-slice_fusion.2
  134.6 3.9 %collective-permute-start = (bf16[15,512]{1,0:T(8,128)(2,1)S(1)}, bf16[15,512]{1,0:T(8,128)(2,1)S(1)}, u32[]{:S(2)}, u32[]{:S(2)}) collective-permute-start(bf16[15,512]{1,0:T(8,128)(2,1)S(1)} %get-tuple-element.99), channel_id=1, source_target_pairs={{0,1},{1,2},{2,3},{3,4},{4,5},{5,6},{6,7},{7,8},{8,9},{9,10},{10,1... | collective-permute-start | bytes 46088 | tf_op jit(solution)/shard_map/ppermute | solution.py:29
  138.5 1.9 %collective-permute-start.1 = (bf16[15,512]{1,0:T(8,128)(2,1)S(1)}, bf16[15,512]{1,0:T(8,128)(2,1)S(1)}, u32[]{:S(2)}, u32[]{:S(2)}) collective-permute-start(bf16[15,512]{1,0:T(8,128)(2,1)S(1)} %get-tuple-element.100), channel_id=1, source_target_pairs={{1,0},{2,1},{3,2},{4,3},{5,4},{6,5},{7,6},{8,7},{9,8},{10,9},{11,1... | collective-permute-start | bytes 46088 | tf_op jit(solution)/shard_map/ppermute | solution.py:32
  140.5 4.0 %collective-permute-done.1 = bf16[15,512]{1,0:T(8,128)(2,1)S(1)} collective-permute-done((bf16[15,512]{1,0:T(8,128)(2,1)S(1)}, bf16[15,512]{1,0:T(8,128)(2,1)S(1)}, u32[]{:S(2)}, u32[]{:S(2)}) %collective-permute-start.1) | collective-permute-done | bytes 15392 | tf_op jit(solution)/shard_map/ppermute | solution.py:32
  144.5 2.0 %fusion.16 = bf16[16,512]{1,0:T(8,128)(2,1)} fusion(f32[16,512]{1,0:T(8,128)S(1)} %get-tuple-element.104, bf16[512,512]{1,0:T(8,128)(2,1)} %param.25, f32[46,512]{1,0:T(8,128)S(1)} %maximum_convert_fusion, f32[512]{0:T(512)S(1)} %copy-done.4, f32[512]{0:T(512)S(1)} %copy-done.5, f32[512]{0:T(512)S(1)} %bitcast.127, f32[512]{0:T(512)S(1)} %bitcast.128, ...), kind=kOutput, calls=%fused_computation.26 | convolution fusion | flops 8962048 | bytes 1656832 | tf_op jit(solution)/shard_map/dot_general | solution.py:124
  (92 shorter events, 9.8 us)
Async XLA Ops:
  6.5 127.7 %copy-start = (bf16[512,1024]{1,0:T(8,128)(2,1)S(1)}, bf16[512,1024]{1,0:T(8,128)(2,1)}, u32[]{:S(2)}) copy-start(bf16[512,1024]{1,0:T(8,128)(2,1)} %param.21) | copy-start | bytes 3145732
  8.1 15.1 %all-to-all-start = ((bf16[16,16,512]{2,1,0:T(8,128)(2,1)}), bf16[16,16,512]{2,1,0:T(8,128)(2,1)S(1)}, u32[]{:S(2)}, u32[]{:S(2)}) async-start(bf16[16,16,512]{2,1,0:T(8,128)(2,1)} %tile.2), calls=%async_computation | async-start | bytes 524288 | tf_op jit(solution)/shard_map/all_to_all | solution.py:13
  14.7 86.4 %all-gather.3.cloned.1.call-start = ((), (), s32[]{:S(2)}) async-start(), calls=%async_computation.1 | async-start | bytes 8912896 | tf_op jit(solution)/shard_map/while/body/eval_jaxpr/all_gather | solution.py:17
  25.6 2.2 %copy-start.2 = (f32[31,512]{1,0:T(8,128)S(1)}, f32[31,512]{1,0:T(8,128)}, u32[]{:S(2)}) copy-start(f32[31,512]{1,0:T(8,128)} %param.22) | copy-start | bytes 190468
  109.9 23.7 %copy-start.1 = (bf16[512,512]{1,0:T(8,128)(2,1)S(1)}, bf16[512,512]{1,0:T(8,128)(2,1)}, u32[]{:S(2)}) copy-start(bf16[512,512]{1,0:T(8,128)(2,1)} %param.20) | copy-start | bytes 1572868
  109.9 23.7 %copy-start.3 = (bf16[16,512]{1,0:T(8,128)(2,1)S(1)}, bf16[16,512]{1,0:T(8,128)(2,1)}, u32[]{:S(2)}) copy-start(bf16[16,512]{1,0:T(8,128)(2,1)} %param.14) | copy-start | bytes 49156
  109.9 34.6 %copy-start.4 = (f32[512]{0:T(512)S(1)}, f32[512]{0:T(512)}, u32[]{:S(2)}) copy-start(f32[512]{0:T(512)} %param.24) | copy-start | bytes 6148
  109.9 34.6 %copy-start.5 = (f32[512]{0:T(512)S(1)}, f32[512]{0:T(512)}, u32[]{:S(2)}) copy-start(f32[512]{0:T(512)} %param.23) | copy-start | bytes 6148
  134.6 5.9 %collective-permute-start = (bf16[15,512]{1,0:T(8,128)(2,1)S(1)}, bf16[15,512]{1,0:T(8,128)(2,1)S(1)}, u32[]{:S(2)}, u32[]{:S(2)}) collective-permute-start(bf16[15,512]{1,0:T(8,128)(2,1)S(1)} %get-tuple-element.99), channel_id=1, source_target_pairs={{0,1},{1,2},{2,3},{3,4},{4,5},{5,6},{6,7},{7,8},{8,9},{9,10},{10,1... | collective-permute-start | bytes 46088 | tf_op jit(solution)/shard_map/ppermute | solution.py:29
  138.5 6.0 %collective-permute-start.1 = (bf16[15,512]{1,0:T(8,128)(2,1)S(1)}, bf16[15,512]{1,0:T(8,128)(2,1)S(1)}, u32[]{:S(2)}, u32[]{:S(2)}) collective-permute-start(bf16[15,512]{1,0:T(8,128)(2,1)S(1)} %get-tuple-element.100), channel_id=1, source_target_pairs={{1,0},{2,1},{3,2},{4,3},{5,4},{6,5},{7,6},{8,7},{9,8},{10,9},{11,1... | collective-permute-start | bytes 46088 | tf_op jit(solution)/shard_map/ppermute | solution.py:32
Sparse Core Ops, SparseCore 0:
  27.9 73.1 all-gather.2
